TPU v7x, 256 devices: a whole 4x4x8 slice. The times are simulated.
256 devices in a mesh: row: 8 (over x, core), col: 32 (over y, z).
Axes of the slice: x: 4, y: 4, z: 8, core: 2. Of those that a mesh axis runs over, the one named last changes fastest.
Arguments:
- inv_diag: float32 [2, 2048, 2048], P(None, 'row', 'col'), may hold values from -1 to 2, as said below
- coupling: float32 [2048, 2048], P('row', 'col'), may hold values from -0.125 to 0.125
- top_rhs: float32 [2, 2048, 4096], P(None, 'row', 'col'), may hold values from -6 to 6
- panel: float32 [2, 8192, 2048], P(None, 'row', 'col'), may hold values from -0.125 to 0.125
- rhs: float32 [8192, 4096], P('row', 'col'), may hold values from -6 to 6
Outputs:
- solved: float32 [2, 2048, 4096], P(None, 'row', 'col')
- trailing: float32 [8192, 4096], P('row', 'col')
Inputs may be any that keep to these rules, and one draw needn't show every extreme that they name: `inv_diag`: each of the two blocks is lower triangular with its diagonal in 1 to 2.
All inputs are finite; a program needn't handle non-finite values.
Results may differ from a plain program's by a relative error of at most 0.000073.
Values sent between devices are 32-bit elements; how exact they have to be, the bound alone decides.
A program may use at most 64 MiB of HBM per device.

v0:
```python
import jax
import jax.numpy as jnp
from jax import lax
from jax.sharding import PartitionSpec as P


def product(left, right):
    return jnp.dot(left, right, precision=lax.Precision.HIGHEST, preferred_element_type=jnp.float32)


def folder(full_rows, piece):
    return product(piece, full_rows)


def body(inv_diag, coupling, top_rhs, panel, rhs):
    first_full_rhs = lax.all_gather(top_rhs[0], "row", axis=0, tiled=True)
    solved_one = folder(first_full_rhs, lax.all_gather(inv_diag[0], "col", axis=1, tiled=True))
    full_one = lax.all_gather(solved_one, "row", axis=0, tiled=True)
    reduced = top_rhs[1] - folder(full_one, lax.all_gather(coupling, "col", axis=1, tiled=True))
    reduced_full = lax.all_gather(reduced, "row", axis=0, tiled=True)
    solved_two = folder(reduced_full, lax.all_gather(inv_diag[1], "col", axis=1, tiled=True))
    full_two = lax.all_gather(solved_two, "row", axis=0, tiled=True)
    solved = jnp.stack([solved_one, solved_two])
    stacked_full = jnp.stack([full_one, full_two])
    update = jnp.einsum(
        "krw,kwt->rt",
        lax.all_gather(panel, "col", axis=2, tiled=True),
        stacked_full,
        precision=lax.Precision.HIGHEST,
        preferred_element_type=jnp.float32,
    )
    trailing = rhs - update
    return (solved, trailing)


def solution(mesh):
    in_specs = (
        P(None, "row", "col"),
        P("row", "col"),
        P(None, "row", "col"),
        P(None, "row", "col"),
        P("row", "col"),
    )
    out_specs = (P(None, "row", "col"), P("row", "col"))
    return jax.shard_map(body, mesh=mesh, in_specs=in_specs, out_specs=out_specs, check_vma=False)
```

profile of v0, /device:TPU:1, one launch (start us, length us, event | category | flops | bytes accessed | tf_op | source)
XLA Modules:
  0.0 524.7 jit_solution(6172325524292058646)
XLA Ops:
  7.2 0.0 copy-start.3
  7.2 0.0 all-gather.24.cloned.1.call-start
  7.2 1.6 slice.13
  8.8 0.0 all-gather.24.cloned.1.call-update
  8.8 0.0 all-gather.22.cloned.1.call-start
  8.9 1.5 fusion.17
  10.4 0.0 all-gather.22.cloned.1.call-update
  10.4 0.0 all-gather.14.cloned.1.call-start
  10.5 0.7 all-gather.14.cloned.1.call-update
  11.2 0.0 all-gather.12.cloned.1.call-start
  11.2 29.2 %all-gather.24.cloned.1.call-done = f32[1,2048,128]{2,1,0:T(8,128)} async-done(((f32[1,256,128]{2,1,0:T(8,128)}), f32[1,2048,128]{2,1,0:T(8,128)}) %all-gather.24.cloned.1.call-update) | async-done | bytes 1048592 | tf_op jit(solution)/shard_map/all_gather | solution.py:16
  40.4 76.0 %all-gather.22.cloned.1.call-done = f32[1,256,2048]{1,2,0:T(8,128)} async-done(((f32[1,256,64]{1,2,0:T(8,128)}), f32[1,256,2048]{1,2,0:T(8,128)}) %all-gather.22.cloned.1.call-update) | async-done | bytes 2097168 | tf_op jit(solution)/shard_map/all_gather | solution.py:17
  116.4 5.9 %fusion.6 = f32[256,128]{1,0:T(8,128)} fusion(f32[1,256,2048]{1,2,0:T(8,128)} %all-gather.22.cloned.1.call-done, f32[1,2048,128]{2,1,0:T(8,128)} %all-gather.24.cloned.1.call-done), kind=kOutput, calls=%fused_computation.6 | convolution fusion | flops 805306368 | bytes 3276800 | tf_op jit(solution)/shard_map/dot_general | solution.py:8
  122.4 0.0 all-gather.12.cloned.1.call-update
  122.4 0.0 all-gather.26.cloned.1.call-start
  122.4 0.5 all-gather.26.cloned.1.call-update
  123.0 0.0 all-gather.16.cloned.1.call-start
  123.0 71.2 %all-gather.14.cloned.1.call-done = f32[256,2048]{0,1:T(8,128)} async-done(((f32[256,64]{0,1:T(8,128)}), f32[256,2048]{0,1:T(8,128)}) %all-gather.14.cloned.1.call-update) | async-done | bytes 2097168 | tf_op jit(solution)/shard_map/all_gather | solution.py:19
  194.2 30.3 %all-gather.12.cloned.1.call-done = f32[2048,128]{1,0:T(8,128)} async-done(((f32[256,128]{1,0:T(8,128)}), f32[2048,128]{1,0:T(8,128)}) %all-gather.12.cloned.1.call-update) | async-done | bytes 1048592 | tf_op jit(solution)/shard_map/all_gather | solution.py:18
  224.5 0.0 copy-done.3
  224.5 6.0 %fusion.14 = f32[256,128]{1,0:T(8,128)} fusion(f32[2048,128]{1,0:T(8,128)} %all-gather.12.cloned.1.call-done, f32[256,2048]{0,1:T(8,128)} %all-gather.14.cloned.1.call-done, f32[2,256,128]{2,1,0:T(8,128)S(1)} %copy-done.3), kind=kOutput, calls=%fused_computation.11 | convolution fusion | flops 805339136 | bytes 3407872 | tf_op jit(solution)/shard_map/dot_general | solution.py:8
  230.5 0.0 copy-start.2
  230.5 0.0 all-gather.16.cloned.1.call-update
  230.5 0.0 copy-start.1
  230.5 0.0 copy-start
  230.5 0.0 all-gather.18.cloned.1.call-start
  230.6 69.2 %all-gather.26.cloned.1.call-done = f32[1,256,2048]{1,2,0:T(8,128)} async-done(((f32[1,256,64]{1,2,0:T(8,128)}), f32[1,256,2048]{1,2,0:T(8,128)}) %all-gather.26.cloned.1.call-update) | async-done | bytes 2097168 | tf_op jit(solution)/shard_map/all_gather | solution.py:21
  299.8 30.3 %all-gather.16.cloned.1.call-done = f32[2048,128]{1,0:T(8,128)} async-done(((f32[256,128]{1,0:T(8,128)}), f32[2048,128]{1,0:T(8,128)}) %all-gather.16.cloned.1.call-update) | async-done | bytes 1048592 | tf_op jit(solution)/shard_map/all_gather | solution.py:20
  330.1 6.0 %fusion.4 = f32[128,256]{0,1:T(8,128)} fusion(f32[2048,128]{1,0:T(8,128)} %all-gather.16.cloned.1.call-done, f32[1,256,2048]{1,2,0:T(8,128)} %all-gather.26.cloned.1.call-done), kind=kOutput, calls=%fused_computation.4 | convolution fusion | flops 805306368 | bytes 3276800 | tf_op jit(solution)/shard_map/dot_general | solution.py:8
  336.1 0.0 all-gather.18.cloned.1.call-update
  336.1 0.2 all-gather.20.cloned.1.call-start
  336.3 0.5 all-gather.20.cloned.1.call-update
  336.9 0.0 copy-done.2
  336.9 0.2 copy.9
  337.1 0.0 copy-done.1
  337.1 1.6 pad_maximum_fusion
  338.7 23.2 %all-gather.18.cloned.1.call-done = f32[2048,128]{1,0:T(8,128)} async-done(((f32[256,128]{1,0:T(8,128)}), f32[2048,128]{1,0:T(8,128)}) %all-gather.18.cloned.1.call-update) | async-done | bytes 1048592 | tf_op jit(solution)/shard_map/all_gather | solution.py:22
  361.9 141.1 %all-gather.20.cloned.1.call-done = f32[2,1024,2048]{1,2,0:T(8,128)} async-done(((f32[2,1024,64]{1,2,0:T(8,128)}), f32[2,1024,2048]{1,2,0:T(8,128)}) %all-gather.20.cloned.1.call-update) | async-done | bytes 16777232 | tf_op jit(solution)/shard_map/all_gather | solution.py:27
  503.0 0.0 copy-done
  503.0 13.8 %fusion.11 = f32[1024,128]{0,1:T(8,128)S(1)} fusion(f32[1024,128]{0,1:T(8,128)S(1)} %copy.9, f32[2,1024,2048]{1,2,0:T(8,128)} %all-gather.20.cloned.1.call-done, f32[1,2048,128]{2,1,0:T(8,128)} %bitcast.35, f32[1,2048,128]{2,1,0:T(8,128)S(1)} %bitcast.31), kind=kOutput, calls=%fused_computation.9 | convolution fusion | flops 6443106304 | bytes 19922944 | tf_op jit(solution)/shard_map/krw,kwt->rt/dot_general | solution.py:25
  516.9 1.0 copy.10
Async XLA Ops:
  7.2 217.3 %copy-start.3 = (f32[2,256,128]{2,1,0:T(8,128)S(1)}, f32[2,256,128]{2,1,0:T(8,128)}, u32[]{:S(2)}) copy-start(f32[2,256,128]{2,1,0:T(8,128)} %param.7) | copy-start | bytes 786436
  7.2 33.2 %all-gather.24.cloned.1.call-start = ((), (), s32[]{:S(2)}) async-start(), calls=%async_computation.6 | async-start | bytes 1179648 | tf_op jit(solution)/shard_map/all_gather | solution.py:16
  8.8 107.6 %all-gather.22.cloned.1.call-start = ((), (), s32[]{:S(2)}) async-start(), calls=%async_computation.5 | async-start | bytes 2162688 | tf_op jit(solution)/shard_map/all_gather | solution.py:17
  10.4 183.7 %all-gather.14.cloned.1.call-start = ((), (), s32[]{:S(2)}) async-start(), calls=%async_computation.1 | async-start | bytes 2162688 | tf_op jit(solution)/shard_map/all_gather | solution.py:19
  11.2 213.3 %all-gather.12.cloned.1.call-start = ((), (), s32[]{:S(2)}) async-start(), calls=%async_computation | async-start | bytes 1179648 | tf_op jit(solution)/shard_map/all_gather | solution.py:18
  122.4 177.4 %all-gather.26.cloned.1.call-start = ((), (), s32[]{:S(2)}) async-start(), calls=%async_computation.7 | async-start | bytes 2162688 | tf_op jit(solution)/shard_map/all_gather | solution.py:21
  123.0 207.1 %all-gather.16.cloned.1.call-start = ((), (), s32[]{:S(2)}) async-start(), calls=%async_computation.2 | async-start | bytes 1179648 | tf_op jit(solution)/shard_map/all_gather | solution.py:20
  230.5 106.4 %copy-start.2 = (f32[1024,128]{1,0:T(8,128)S(1)}, f32[1024,128]{1,0:T(8,128)}, u32[]{:S(2)}) copy-start(f32[1024,128]{1,0:T(8,128)} %param.9) | copy-start | bytes 1572868
  230.5 106.6 %copy-start.1 = (f32[256,128]{1,0:T(8,128)S(1)}, f32[256,128]{1,0:T(8,128)}, u32[]{:S(2)}) copy-start(f32[256,128]{1,0:T(8,128)} %fusion.6) | copy-start | bytes 393220
  230.5 272.5 %copy-start = (f32[2048,128]{1,0:T(8,128)S(1)}, f32[2048,128]{1,0:T(8,128)}, u32[]{:S(2)}) copy-start(f32[2048,128]{1,0:T(8,128)} %all-gather.12.cloned.1.call-done) | copy-start | bytes 3145732
  230.5 131.4 %all-gather.18.cloned.1.call-start = ((), (), s32[]{:S(2)}) async-start(), calls=%async_computation.3 | async-start | bytes 1179648 | tf_op jit(solution)/shard_map/all_gather | solution.py:22
  336.1 166.9 %all-gather.20.cloned.1.call-start = ((), (), s32[]{:S(2)}) async-start(), calls=%async_computation.4 | async-start | bytes 17301504 | tf_op jit(solution)/shard_map/all_gather | solution.py:27
Sparse Core Ops, SparseCore 0:
  10.4 29.9 all-gather.23
  43.6 72.8 all-gather.21
  119.0 75.1 all-gather.13
  196.5 27.9 all-gather.11
  226.9 72.8 all-gather.25
  302.1 27.9 all-gather.15
  336.2 25.6 all-gather.17
  364.5 138.4 all-gather.19
where the time goes:
time: 525 us
  waiting for transfers between devices  472 us (90%)
  matrix products  31.8 us (6%)
  between operations  14.2 us (3%)
    all_gather x1, waiting for transfers between devices, body(): lax.all_gather(panel, 'col', axis=2, tiled=True)  141 us
    all_gather x1, waiting for transfers between devices, body(): lax.all_gather(inv_diag[0], 'col', axis=1, tiled=True)  76 us
    all_gather x1, waiting for transfers between devices, body(): lax.all_gather(coupling, 'col', axis=1, tiled=True)  71.2 us
    all_gather x1, waiting for transfers between devices, body(): lax.all_gather(inv_diag[1], 'col', axis=1, tiled=True)  69.2 us
    all_gather x1, waiting for transfers between devices, body(): full_one = lax.all_gather(solved_one, 'row', axis=0, tiled=True)  30.3 us
    all_gather x1, waiting for transfers between devices, body(): reduced_full = lax.all_gather(reduced, 'row', axis=0, tiled=True)  30.3 us
    all_gather x1, waiting for transfers between devices, body(): first_full_rhs = lax.all_gather(top_rhs[0], 'row', axis=0, tiled=True)  29.2 us
    all_gather x1, waiting for transfers between devices, body(): full_two = lax.all_gather(solved_two, 'row', axis=0, tiled=True)  23.2 us
  transfers between devices with their start and end apart: 8, of which 8 were waited for; matrix products, arithmetic and copies ran while one was open for 3% of the time, Pallas kernels for 0%

commit v1 on v0

--- a/solution.py
+++ b/solution.py
@@ -17,7 +17,10 @@
     solved_one = folder(first_full_rhs, lax.all_gather(inv_diag[0], "col", axis=1, tiled=True))
     full_one = lax.all_gather(solved_one, "row", axis=0, tiled=True)
     reduced = top_rhs[1] - folder(full_one, lax.all_gather(coupling, "col", axis=1, tiled=True))
-    reduced_full = lax.all_gather(reduced, "row", axis=0, tiled=True)
+    peers = lax.axis_size("row")
+    pieces = jnp.stack([reduced for _ in range(peers)])
+    pieces = lax.all_to_all(pieces, "row", split_axis=0, concat_axis=0)
+    reduced_full = jnp.concatenate(pieces, axis=0)
     solved_two = folder(reduced_full, lax.all_gather(inv_diag[1], "col", axis=1, tiled=True))
     full_two = lax.all_gather(solved_two, "row", axis=0, tiled=True)
     solved = jnp.stack([solved_one, solved_two])

time: 525 us -> 497 us (0.947)
  waiting for transfers between devices: 472 us -> 442 us
    all_gather x1 -> x0, waiting for transfers between devices: 30.3 us -> none  [body(): reduced_full = lax.all_gather(reduced, 'row', axis=0, tiled=True)]
  transfers between devices with their start and end apart: 8 -> 8, of which waited for: 8 -> 7; matrix products, arithmetic and copies ran while one was open for 3% -> 3% of each run, Pallas kernels for 0% -> 0%
where the time goes in v1:
time: 497 us
  waiting for transfers between devices  442 us (89%)
  matrix products  29.3 us (6%)
  between operations  14.2 us (3%)
  local copies, waits for them, and re-layouts  5.63 us (1%)
    all_gather x1, waiting for transfers between devices, body(): lax.all_gather(panel, 'col', axis=2, tiled=True)  141 us
    all_gather x1, waiting for transfers between devices, body(): lax.all_gather(inv_diag[0], 'col', axis=1, tiled=True)  75.5 us
    all_gather x1, waiting for transfers between devices, body(): lax.all_gather(coupling, 'col', axis=1, tiled=True)  71.1 us
    all_gather x1, waiting for transfers between devices, body(): lax.all_gather(inv_diag[1], 'col', axis=1, tiled=True)  67.2 us
    all_gather x1, waiting for transfers between devices, body(): full_one = lax.all_gather(solved_one, 'row', axis=0, tiled=True)  30.3 us
    all_gather x1, waiting for transfers between devices, body(): first_full_rhs = lax.all_gather(top_rhs[0], 'row', axis=0, tiled=True)  29.1 us
    all_gather x1, waiting for transfers between devices, body(): full_two = lax.all_gather(solved_two, 'row', axis=0, tiled=True)  25.5 us
    dot_general x3, matrix products, product(): jnp.dot(left, right, precision=lax.Precision.HIGHEST, preferred_element_t...  15.5 us
  transfers between devices with their start and end apart: 8, of which 7 were waited for; matrix products, arithmetic and copies ran while one was open for 3% of the time, Pallas kernels for 0%

profile of v1, /device:TPU:1, one launch (start us, length us, event | category | flops | bytes accessed | tf_op | source)
XLA Modules:
  0.0 496.5 jit_solution(9042975663062007161)
XLA Ops:
  7.2 0.0 all-gather.21.cloned.1.call-start
  7.2 1.6 fusion.17
  8.9 0.0 all-gather.21.cloned.1.call-update
  8.9 0.0 all-gather.19.cloned.1.call-start
  8.9 1.5 fusion.18
  10.4 0.0 all-gather.19.cloned.1.call-update
  10.5 0.0 all-gather.13.cloned.1.call-start
  10.5 0.7 all-gather.13.cloned.1.call-update
  11.2 0.0 all-gather.11.cloned.1.call-start
  11.3 29.1 %all-gather.21.cloned.1.call-done = f32[1,2048,128]{2,1,0:T(8,128)} async-done(((f32[1,256,128]{2,1,0:T(8,128)}), f32[1,2048,128]{2,1,0:T(8,128)}) %all-gather.21.cloned.1.call-update) | async-done | bytes 1048592 | tf_op jit(solution)/shard_map/all_gather | solution.py:16
  40.4 75.5 %all-gather.19.cloned.1.call-done = f32[1,256,2048]{1,2,0:T(8,128)} async-done(((f32[1,256,64]{1,2,0:T(8,128)}), f32[1,256,2048]{1,2,0:T(8,128)}) %all-gather.19.cloned.1.call-update) | async-done | bytes 2097168 | tf_op jit(solution)/shard_map/all_gather | solution.py:17
  115.8 5.9 %fusion.6 = f32[256,128]{1,0:T(8,128)} fusion(f32[1,256,2048]{1,2,0:T(8,128)} %all-gather.19.cloned.1.call-done, f32[1,2048,128]{2,1,0:T(8,128)} %all-gather.21.cloned.1.call-done), kind=kOutput, calls=%fused_computation.6 | convolution fusion | flops 805306368 | bytes 3276800 | tf_op jit(solution)/shard_map/dot_general | solution.py:8
  121.8 0.0 all-gather.11.cloned.1.call-update
  121.8 0.0 all-gather.23.cloned.1.call-start
  121.8 0.5 all-gather.23.cloned.1.call-update
  122.4 0.1 copy.15
  122.5 71.1 %all-gather.13.cloned.1.call-done = f32[256,2048]{0,1:T(8,128)} async-done(((f32[256,64]{0,1:T(8,128)}), f32[256,2048]{0,1:T(8,128)}) %all-gather.13.cloned.1.call-update) | async-done | bytes 2097168 | tf_op jit(solution)/shard_map/all_gather | solution.py:19
  193.6 30.3 %all-gather.11.cloned.1.call-done = f32[2048,128]{1,0:T(8,128)} async-done(((f32[256,128]{1,0:T(8,128)}), f32[2048,128]{1,0:T(8,128)}) %all-gather.11.cloned.1.call-update) | async-done | bytes 1048592 | tf_op jit(solution)/shard_map/all_gather | solution.py:18
  223.9 3.8 fusion.14
  227.7 0.1 copy.8
  227.8 1.1 stack.30
  228.9 3.7 all-to-all-start
  232.6 0.0 copy-start.2
  232.6 0.0 all-gather.15.cloned.1.call-start
  232.6 67.2 %all-gather.23.cloned.1.call-done = f32[1,256,2048]{1,2,0:T(8,128)} async-done(((f32[1,256,64]{1,2,0:T(8,128)}), f32[1,256,2048]{1,2,0:T(8,128)}) %all-gather.23.cloned.1.call-update) | async-done | bytes 2097168 | tf_op jit(solution)/shard_map/all_gather | solution.py:24
  299.8 0.0 all-to-all-done
  299.8 0.0 copy-start.1
  299.8 0.0 copy-start
  299.8 5.8 %fusion.4 = f32[128,256]{0,1:T(8,128)} fusion(f32[2048,128]{1,0:T(8,128)S(1)} %bitcast.33, f32[1,256,2048]{1,2,0:T(8,128)} %all-gather.23.cloned.1.call-done), kind=kOutput, calls=%fused_computation.4 | convolution fusion | flops 805306368 | bytes 3276800 | tf_op jit(solution)/shard_map/dot_general | solution.py:8
  305.6 0.0 all-gather.15.cloned.1.call-update
  305.6 0.2 all-gather.17.cloned.1.call-start
  305.8 0.5 all-gather.17.cloned.1.call-update
  306.3 0.0 copy-done.2
  306.3 0.2 copy.11
  306.5 0.0 copy-done.1
  306.6 1.6 pad_maximum_fusion
  308.2 25.5 %all-gather.15.cloned.1.call-done = f32[2048,128]{1,0:T(8,128)} async-done(((f32[256,128]{1,0:T(8,128)}), f32[2048,128]{1,0:T(8,128)}) %all-gather.15.cloned.1.call-update) | async-done | bytes 1048592 | tf_op jit(solution)/shard_map/all_gather | solution.py:25
  333.7 141.1 %all-gather.17.cloned.1.call-done = f32[2,1024,2048]{1,2,0:T(8,128)} async-done(((f32[2,1024,64]{1,2,0:T(8,128)}), f32[2,1024,2048]{1,2,0:T(8,128)}) %all-gather.17.cloned.1.call-update) | async-done | bytes 16777232 | tf_op jit(solution)/shard_map/all_gather | solution.py:30
  474.8 0.0 copy-done
  474.8 13.8 %fusion.11 = f32[1024,128]{0,1:T(8,128)S(1)} fusion(f32[1024,128]{0,1:T(8,128)S(1)} %copy.11, f32[2,1024,2048]{1,2,0:T(8,128)} %all-gather.17.cloned.1.call-done, f32[1,2048,128]{2,1,0:T(8,128)} %bitcast.37, f32[1,2048,128]{2,1,0:T(8,128)S(1)} %bitcast.32), kind=kOutput, calls=%fused_computation.9 | convolution fusion | flops 6443106304 | bytes 19922944 | tf_op jit(solution)/shard_map/krw,kwt->rt/dot_general | solution.py:28
  488.7 1.0 copy.12
Async XLA Ops:
  7.2 33.2 %all-gather.21.cloned.1.call-start = ((), (), s32[]{:S(2)}) async-start(), calls=%async_computation.6 | async-start | bytes 1179648 | tf_op jit(solution)/shard_map/all_gather | solution.py:16
  8.9 107.0 %all-gather.19.cloned.1.call-start = ((), (), s32[]{:S(2)}) async-start(), calls=%async_computation.5 | async-start | bytes 2162688 | tf_op jit(solution)/shard_map/all_gather | solution.py:17
  10.5 183.1 %all-gather.13.cloned.1.call-start = ((), (), s32[]{:S(2)}) async-start(), calls=%async_computation.2 | async-start | bytes 2162688 | tf_op jit(solution)/shard_map/all_gather | solution.py:19
  11.2 212.7 %all-gather.11.cloned.1.call-start = ((), (), s32[]{:S(2)}) async-start(), calls=%async_computation.1 | async-start | bytes 1179648 | tf_op jit(solution)/shard_map/all_gather | solution.py:18
  121.8 178.0 %all-gather.23.cloned.1.call-start = ((), (), s32[]{:S(2)}) async-start(), calls=%async_computation.7 | async-start | bytes 2162688 | tf_op jit(solution)/shard_map/all_gather | solution.py:24
  228.9 70.9 %all-to-all-start = ((f32[8,256,128]{2,1,0:T(8,128)}), f32[8,256,128]{2,1,0:T(8,128)S(1)}, u32[]{:S(2)}, u32[]{:S(2)}) async-start(f32[8,256,128]{2,1,0:T(8,128)} %stack.30), calls=%async_computation | async-start | bytes 2097152 | tf_op jit(solution)/shard_map/all_to_all | solution.py:22
  232.6 73.7 %copy-start.2 = (f32[1024,128]{1,0:T(8,128)S(1)}, f32[1024,128]{1,0:T(8,128)}, u32[]{:S(2)}) copy-start(f32[1024,128]{1,0:T(8,128)} %param.9) | copy-start | bytes 1572868
  232.6 101.1 %all-gather.15.cloned.1.call-start = ((), (), s32[]{:S(2)}) async-start(), calls=%async_computation.3 | async-start | bytes 1179648 | tf_op jit(solution)/shard_map/all_gather | solution.py:25
  299.8 6.8 %copy-start.1 = (f32[256,128]{1,0:T(8,128)S(1)}, f32[256,128]{1,0:T(8,128)}, u32[]{:S(2)}) copy-start(f32[256,128]{1,0:T(8,128)} %fusion.6) | copy-start | bytes 393220
  299.8 175.0 %copy-start = (f32[2048,128]{1,0:T(8,128)S(1)}, f32[2048,128]{1,0:T(8,128)}, u32[]{:S(2)}) copy-start(f32[2048,128]{1,0:T(8,128)} %all-gather.11.cloned.1.call-done) | copy-start | bytes 3145732
  305.6 169.2 %all-gather.17.cloned.1.call-start = ((), (), s32[]{:S(2)}) async-start(), calls=%async_computation.4 | async-start | bytes 17301504 | tf_op jit(solution)/shard_map/all_gather | solution.py:30
Sparse Core Ops, SparseCore 0:
  10.4 29.9 all-gather.20
  43.0 72.8 all-gather.18
  118.4 75.1 all-gather.12
  195.9 27.9 all-gather.10
  226.9 72.8 all-gather.22
  305.7 27.9 all-gather.14
  336.3 138.4 all-gather.16
